TPU v7x, 32 devices: a whole 2x2x4 slice. The times are simulated.
32 devices in a mesh: cl: 8 (over z, x), grp: 4 (over y, core).
Axes of the slice: x: 2, y: 2, z: 4, core: 2. Of those that a mesh axis runs over, the one named last changes fastest.
Arguments:
- basis: float32 [16, 4, 64, 128], P(None, 'grp', 'cl'), may hold values from -6 to 6
- near_blocks: bfloat16 [4, 64, 4, 128, 128], P('grp', 'cl'), may hold values from -0.25 to 0.25
- near_list: int32 [4, 64, 4], P('grp', 'cl'), may hold values from 0 to 23
- source_basis: bfloat16 [4, 64, 32, 128], P('grp', 'cl'), may hold values from -0.5 to 0.5
- target_basis: bfloat16 [4, 64, 32, 128], P('grp', 'cl'), may hold values from -1 to 1
- coupling: bfloat16 [4, 128, 1024], P('grp', 'cl'), may hold values from -0.75 to 0.75
- far_target: int32 [4, 128], P('grp'), may hold values from 0 to 63, as said below
- far_source: int32 [4, 128], P('grp', 'cl'), may hold values from 0 to 63, as said below
- far_count: int32 [4, 8], P('grp', 'cl'), may hold values from 8 to 16
Outputs:
- next_vector: float32 [4, 64, 128], P('grp', 'cl')
- hessenberg: float32 [17], replicated
Inputs may be any that keep to these rules, and one draw needn't show every extreme that they name: `far_target`: slots are owned in blocks of 16, block d by owner d of the group, whose clusters are d * 8 to (d + 1) * 8 - 1. Except for slot 1 of each owner, a slot's target lies within 16 clusters before or 23 after the owner's first cluster. Slot 1's target is a cluster of owner (d + 4) % 8. `far_source`: except for slot 0 of each owner, a slot's source lies within 80 clusters before or 87 after the owner's first cluster, and where the slot's target obeys the rule above the source differs from it by 16 to 64 clusters. Slot 0's source is a cluster of owner (d + 4) % 8.
All inputs are finite; a program needn't handle non-finite values.
Results may differ from a plain program's by a relative error of at most 0.0039.
Values may be sent and summed in bfloat16 or wider, within the bound.
A program may use at most 64 MiB of HBM per device.

v0:
```python
import jax
import jax.numpy as jnp
from jax import lax
from jax.sharding import PartitionSpec as P


def with_halo(cells, sides, width):
    for axis, dim in sides:
        count = lax.axis_size(axis)
        ends = count - 1
        head = lax.slice_in_dim(cells, 0, width, axis=dim)
        tail = lax.slice_in_dim(cells, cells.shape[dim] - width, cells.shape[dim], axis=dim)
        cells = jnp.concatenate(
            [
                lax.ppermute(tail, axis, [(i, (i + 1) % count) for i in range(ends)]),
                cells,
                lax.ppermute(head, axis, [((i + 1) % count, i) for i in range(ends)]),
            ],
            axis=dim,
        )
    return cells


def on_device(
    basis,
    near_blocks,
    near_list,
    source_basis,
    target_basis,
    coupling,
    far_target,
    far_source,
    far_count,
):
    basis_count = basis.shape[0]
    clusters = basis.shape[2]
    panels_cl = basis.shape[3]
    ranks = source_basis.shape[2]
    block_slots = coupling.shape[1]
    current = basis[basis_count - 1, 0]
    current_bf = current.astype(jnp.bfloat16)
    window = with_halo(current_bf, (("cl", 0),), clusters)
    gathered = window[near_list[0]]
    near_part = jnp.einsum(
        "tkij,tkj->ti", near_blocks[0], gathered, preferred_element_type=jnp.float32
    )
    expansion = jnp.einsum(
        "srp,sp->sr", source_basis[0], current_bf, preferred_element_type=jnp.float32
    ).astype(jnp.bfloat16)
    my_index = lax.axis_index("cl")
    slot_local = jnp.arange(block_slots, dtype=jnp.int32)
    my_sources = far_source[0]
    all_expansion = lax.all_gather(expansion, "cl", axis=0, tiled=True)
    picked = all_expansion[my_sources]
    square_blocks = coupling[0].reshape(block_slots, ranks, ranks)
    live_mask = (slot_local < far_count[0, 0]).astype(jnp.float32)
    contributions = (
        jnp.einsum("bij,bj->bi", square_blocks, picked, preferred_element_type=jnp.float32)
        * live_mask[:, None]
    )
    my_targets = lax.dynamic_slice_in_dim(far_target[0], my_index * block_slots, block_slots)
    row_ids = jnp.arange(clusters * lax.axis_size("cl"), dtype=jnp.int32)
    selector = (row_ids[:, None] == my_targets[None, :]).astype(jnp.float32)
    coupled = lax.psum_scatter(
        jnp.dot(selector, contributions, precision=lax.Precision.HIGHEST),
        "cl",
        scatter_dimension=0,
        tiled=True,
    )
    coupled_bf = coupled.astype(jnp.bfloat16)
    far_part = jnp.einsum(
        "tr,trp->tp", coupled_bf, target_basis[0], preferred_element_type=jnp.float32
    )
    image = 0.5 * current + near_part + far_part
    flat_basis = basis[:, 0].reshape(basis_count, clusters * panels_cl)
    flat_image = image.reshape(-1)
    panels = float(lax.axis_size("cl") * lax.axis_size("grp") * clusters * panels_cl)
    local_products = jnp.dot(flat_basis, flat_image, precision=lax.Precision.HIGHEST)
    gram_local = jnp.dot(flat_basis, flat_basis.T, precision=lax.Precision.HIGHEST)
    products, image_squares, gram_matrix = lax.psum(
        (local_products, jnp.sum(flat_image * flat_image), gram_local), ("cl", "grp")
    )
    projection = products / panels
    remainder = flat_image - jnp.dot(projection, flat_basis, precision=lax.Precision.HIGHEST)
    squares = (
        image_squares
        - 2.0 * jnp.sum(projection * products)
        + jnp.dot(
            projection,
            jnp.dot(gram_matrix, projection, precision=lax.Precision.HIGHEST),
            precision=lax.Precision.HIGHEST,
        )
    )
    new_norm = jnp.sqrt(squares / panels + 1e-06)
    next_vector = (remainder / new_norm).reshape(1, clusters, panels_cl)
    return (next_vector, jnp.concatenate([projection, new_norm[None]]))


def solution(mesh):
    placed = (
        P(None, "grp", "cl", None),
        P("grp", "cl", None, None, None),
        P("grp", "cl", None),
        P("grp", "cl", None, None),
        P("grp", "cl", None, None),
        P("grp", "cl", None),
        P("grp", None),
        P("grp", "cl"),
        P("grp", "cl"),
    )
    return jax.shard_map(
        on_device,
        mesh=mesh,
        in_specs=placed,
        out_specs=(P("grp", "cl", None), P()),
        check_vma=False,
    )
```

profile of v0, /device:TPU:0, one launch (start us, length us, event | category | flops | bytes accessed | tf_op | source)
XLA Modules:
  0.0 121.3 jit_solution(2837860129529427694)
XLA Ops:
  0.6 0.0 copy-start
  0.6 0.8 fusion.28
  1.4 4.9 %collective-permute-start = (bf16[8,128]{1,0:T(8,128)(2,1)S(1)}, bf16[8,128]{1,0:T(8,128)(2,1)S(1)}, u32[]{:S(2)}, u32[]{:S(2)}) collective-permute-start(bf16[8,128]{1,0:T(8,128)(2,1)S(1)} %get-tuple-element.7), channel_id=1, source_target_pairs={{0,4},{4,8},{8,12},{12,16},{16,20},{20,24},{24,28},{1,5},{5,9},{9,... | collective-permute-start | bytes 6152 | tf_op jit(solution)/shard_map/ppermute | solution.py:15
  6.3 1.3 %collective-permute-start.1 = (bf16[8,128]{1,0:T(8,128)(2,1)S(1)}, bf16[8,128]{1,0:T(8,128)(2,1)S(1)}, u32[]{:S(2)}, u32[]{:S(2)}) collective-permute-start(bf16[8,128]{1,0:T(8,128)(2,1)S(1)} %get-tuple-element.7), channel_id=1, source_target_pairs={{4,0},{8,4},{12,8},{16,12},{20,16},{24,20},{28,24},{5,1},{9,5},{13... | collective-permute-start | bytes 6152 | tf_op jit(solution)/shard_map/ppermute | solution.py:17
  7.6 0.0 copy-start.3
  7.6 0.7 copy-done.3
  8.3 0.1 copy.13
  8.4 0.1 reshape.85
  8.5 0.0 copy-start.5
  8.5 1.0 fusion.9
  9.4 0.0 copy-start.2
  9.4 28.6 %all_gather.3 = bf16[64,32]{1,0:T(8,128)(2,1)S(1)} all-gather(bf16[8,32]{1,0:T(8,128)(2,1)S(1)} %convert_element_type.22), channel_id=1, replica_groups=mesh['cl'=8,'grp'=4] {'cl'}, dimensions={0}, use_global_device_ids=true | all-gather | bytes 4608 | tf_op jit(solution)/shard_map/all_gather | solution.py:53
  38.1 0.0 copy-done.5
  38.1 0.0 copy-done.2
  38.1 0.1 reshape_squeeze.6
  38.9 0.0 copy-start.6
  39.0 0.6 copy-done.6
  39.6 0.1 dynamic-slice_bitcast_fusion
  39.7 0.6 gather_fusion.1
  40.2 0.2 fusion.17
  40.4 0.0 copy-start.1
  40.4 0.2 fusion.14
  40.6 0.0 copy-start.4
  40.7 34.8 %all-reduce = bf16[64,32]{1,0:T(8,128)(2,1)S(1)} all-reduce(f32[64,32]{1,0:T(8,128)S(1)} %fusion.14), channel_id=2, replica_groups=mesh['cl'=8,'grp'=4] {'cl'}, use_global_device_ids=true, to_apply=%region_0.0.clone | all-reduce | flops 2048 | bytes 12288
  75.4 0.0 copy-done.1
  75.5 0.2 convolution_bitcast_fusion
  75.6 0.0 copy-start.7
  75.6 0.7 copy-done.7
  76.3 0.6 dynamic-slice.1
  77.6 0.0 copy-done.4
  77.6 0.1 fusion.7
  77.7 0.0 collective-permute-done
  77.7 0.0 collective-permute-done.1
  77.8 0.6 gather_fusion
  78.3 0.0 copy-done
  78.4 0.4 fusion.1
  78.7 0.6 multiply_reduce_fusion
  79.3 0.1 convolution_bitcast_fusion.2
  79.5 37.0 %all-reduce.1 = (f32[16]{0:T(128)S(1)}, f32[]{:T(128)}, f32[16,16]{1,0:T(8,128)S(1)}) all-reduce(f32[16]{0:T(128)S(1)} %convolution_bitcast_fusion.2, f32[]{:T(128)} %get-tuple-element.5, f32[16,16]{1,0:T(8,128)S(1)} %convolution_bitcast_fusion), channel_id=1, replica_groups=mesh['cl'=8,'grp'=4] {'cl','grp'}, use_global_device_ids=true, to_apply=%region_1.0 | all-reduce | flops 273 | bytes 2184 | tf_op jit(solution)/shard_map/psum | solution.py:80
  116.5 0.6 broadcast_multiply_fusion
  117.1 0.2 fusion.4
  117.3 0.8 fusion.3
  120.1 0.6 fusion.21
  120.7 0.6 pad_maximum_fusion.1
  (8 shorter events, 0.0 us)
Async XLA Ops:
  0.6 77.7 %copy-start = (bf16[1,8,4,128,128]{4,3,2,1,0:T(8,128)(2,1)S(1)}, bf16[1,8,4,128,128]{4,3,2,1,0:T(8,128)(2,1)}, u32[]{:S(2)}) copy-start(bf16[1,8,4,128,128]{4,3,2,1,0:T(8,128)(2,1)} %param.10) | copy-start | bytes 3145732
  1.4 76.3 %collective-permute-start = (bf16[8,128]{1,0:T(8,128)(2,1)S(1)}, bf16[8,128]{1,0:T(8,128)(2,1)S(1)}, u32[]{:S(2)}, u32[]{:S(2)}) collective-permute-start(bf16[8,128]{1,0:T(8,128)(2,1)S(1)} %get-tuple-element.7), channel_id=1, source_target_pairs={{0,4},{4,8},{8,12},{12,16},{16,20},{20,24},{24,28},{1,5},{5,9},{9,... | collective-permute-start | bytes 6152 | tf_op jit(solution)/shard_map/ppermute | solution.py:15
  6.3 71.4 %collective-permute-start.1 = (bf16[8,128]{1,0:T(8,128)(2,1)S(1)}, bf16[8,128]{1,0:T(8,128)(2,1)S(1)}, u32[]{:S(2)}, u32[]{:S(2)}) collective-permute-start(bf16[8,128]{1,0:T(8,128)(2,1)S(1)} %get-tuple-element.7), channel_id=1, source_target_pairs={{4,0},{8,4},{12,8},{16,12},{20,16},{24,20},{28,24},{5,1},{9,5},{13... | collective-permute-start | bytes 6152 | tf_op jit(solution)/shard_map/ppermute | solution.py:17
  7.6 0.7 copy-start.3
  8.5 29.6 %copy-start.5 = (s32[1,16]{1,0:T(1,128)S(1)}, s32[1,16]{1,0:T(1,128)}, u32[]{:S(2)}) copy-start(s32[1,16]{1,0:T(1,128)} %param.16) | copy-start | bytes 196
  9.4 28.7 %copy-start.2 = (bf16[1,16,1024]{2,1,0:T(8,128)(2,1)S(1)}, bf16[1,16,1024]{2,1,0:T(8,128)(2,1)}, u32[]{:S(2)}) copy-start(bf16[1,16,1024]{2,1,0:T(8,128)(2,1)} %param.14) | copy-start | bytes 98308
  38.9 0.7 copy-start.6
  40.4 35.0 %copy-start.1 = (f32[16,1,8,128]{3,2,1,0:T(8,128)S(1)}, f32[16,1,8,128]{3,2,1,0:T(8,128)}, u32[]{:S(2)}) copy-start(f32[16,1,8,128]{3,2,1,0:T(8,128)} %param.9) | copy-start | bytes 196612
  40.6 36.9 %copy-start.4 = (bf16[1,8,32,128]{3,2,1,0:T(8,128)(2,1)S(1)}, bf16[1,8,32,128]{3,2,1,0:T(8,128)(2,1)}, u32[]{:S(2)}) copy-start(bf16[1,8,32,128]{3,2,1,0:T(8,128)(2,1)} %param.13) | copy-start | bytes 196612
  75.6 0.7 copy-start.7
where the time goes:
time: 123 us; the launch traced here: 121 us
  blocking collectives  100 us (81%)
  starting transfers between devices  6.15 us (5%)
  local copies, waits for them, and re-layouts  4.96 us (4%)
  between operations  4.13 us (3%)
  matrix products  3.17 us (3%)
  other arithmetic  2.44 us (2%)
    psum x1, blocking collectives, on_device(): lax.psum((local_products, jnp.sum(flat_image * flat_image), gram_local),...  37 us
    unnamed x1, blocking collectives  34.8 us
    all_gather x1, blocking collectives, on_device(): all_expansion = lax.all_gather(expansion, 'cl', axis=0, tiled=True)  28.6 us
    ppermute x1, starting transfers between devices, with_halo(): lax.ppermute(tail, axis, [(i, (i + 1) % count) for i in range(ends)])  4.86 us
    unnamed x17, local copies, waits for them, and re-layouts  2.62 us
  transfers between devices with their start and end apart: 2, of which 0 were waited for; matrix products, arithmetic and copies ran while one was open for 3% of the time, Pallas kernels for 0%

commit v1 on v0

v1 whole, which is shorter than its diff:
```python
import functools

import jax
import jax.numpy as jnp
from jax import lax
from jax.experimental import pallas as pl
from jax.experimental.pallas import tpu as pltpu
from jax.sharding import PartitionSpec as P

MESH = pl.DeviceIdType.MESH
TARGET_REACH = 2


def target_offsets(n_cl):
    near = {o % n_cl for r in range(1, TARGET_REACH + 1) for o in (r, -r)}
    return sorted((near | {n_cl // 2}) - {0})


def iota(shape, dim):
    return lax.broadcasted_iota(jnp.int32, shape, dim)


def parts3(x):
    hi = x.astype(jnp.bfloat16)
    rest = x - hi.astype(jnp.float32)
    mid = rest.astype(jnp.bfloat16)
    lo = (rest - mid.astype(jnp.float32)).astype(jnp.bfloat16)
    return hi, mid, lo


def dot_t(a, b):
    return lax.dot_general(a, b, (((1,), (1,)), ((), ())), preferred_element_type=jnp.float32)


def dot(a, b):
    return jnp.dot(a, b, preferred_element_type=jnp.float32)


def kernel(
    n_cl,
    n_grp,
    offsets,
    basis_h,
    near_h,
    list_h,
    sb_h,
    tb_h,
    coup_h,
    ft_h,
    fs_h,
    fc_h,
    out_ref,
    hess_ref,
    bv,
    nv,
    lv,
    sbv,
    tbv,
    cv,
    ftv,
    fsv,
    fcv,
    spread,
    gather,
    e_send,
    e_recv,
    halo,
    p_send,
    p_recv,
    ga_send,
    ga_recv,
    gb_send,
    gb_recv,
    r_send,
    r_recv,
    local_sem,
    halo_sem,
    send_sem,
    recv_sem,
):
    f32, bf16 = jnp.float32, jnp.bfloat16
    me, grp = lax.axis_index("cl"), lax.axis_index("grp")
    total = n_cl * n_grp
    flat_me = me * n_grp + grp
    clusters, near_k = lv.shape
    width = bv.shape[1]
    count = bv.shape[0] // clusters
    slots = cv.shape[0]
    ranks = sbv.shape[0] // clusters
    wide = clusters * ranks
    all_cl = n_cl * clusters

    barrier = pltpu.get_barrier_semaphore()

    def far_device(o):
        flat = lax.rem(flat_me + o, total)
        return {"cl": lax.div(flat, n_grp), "grp": lax.rem(flat, n_grp)}

    def greet(o, _):
        pl.semaphore_signal(barrier, inc=1, device_id=far_device(o), device_id_type=MESH)
        return 0

    loads = [
        pltpu.make_async_copy(src, dst, local_sem.at[i])
        for i, (src, dst) in enumerate(
            [
                (basis_h, bv),
                (sb_h, sbv),
                (coup_h, cv),
                (ft_h, ftv),
                (fs_h, fsv),
                (fc_h, fcv),
                (list_h, lv),
                (near_h, nv),
                (tb_h, tbv),
            ]
        )
    ]
    for load in loads:
        load.start()
    lax.fori_loop(1, total, greet, 0)

    loads[0].wait()
    loads[1].wait()
    current = bv[(count - 1) * clusters :, :]
    current_bf = current.astype(bf16)
    own_lane = iota((clusters, wide), 0) == lax.div(iota((clusters, wide), 1), ranks)
    e8 = jnp.where(own_lane, dot_t(current_bf, sbv[...]), 0.0)
    e_send[0] = jnp.sum(e8, axis=0, keepdims=True).astype(bf16).astype(f32)

    pl.semaphore_wait(barrier, total - 1)

    def send(src, dst, which, device):
        return pltpu.make_async_remote_copy(
            src_ref=src,
            dst_ref=dst,
            send_sem=send_sem.at[which],
            recv_sem=recv_sem.at[which],
            device_id=device,
            device_id_type=MESH,
        )

    def send_e(o, _):
        send(e_send, e_recv.at[pl.ds(o - 1, 1)], 0, {"cl": lax.rem(me + o, n_cl)}).start()
        return 0

    lax.fori_loop(1, n_cl, send_e, 0)
    tile = bv.at[pl.ds((count - 1) * clusters, clusters)]
    halos = [
        pltpu.make_async_remote_copy(
            src_ref=tile,
            dst_ref=halo.at[i],
            send_sem=halo_sem.at[i],
            recv_sem=halo_sem.at[2 + i],
            device_id={"cl": lax.rem(me + shift, n_cl)},
            device_id_type=MESH,
        )
        for i, shift in enumerate((1, n_cl - 1))
    ]
    for copy in halos:
        copy.start()

    def fill(ref, test):
        step = 128
        for at in range(0, ref.shape[0], step):
            block = (step, ref.shape[1])
            ref[at : at + step, :] = jnp.where(test(iota(block, 0) + at, iota(block, 1)), 1.0, 0.0).astype(bf16)

    fill(spread, lambda r, c: lax.rem(r, ranks) == lax.rem(c, ranks))
    fill(gather, lambda r, c: lax.div(r, ranks) == lax.rem(c, ranks))

    for load in loads[2:6]:
        load.wait()
    eye = iota((slots, slots), 0) == iota((slots, slots), 1)
    sources = jnp.sum(jnp.where(eye, fsv[...], 0), axis=1, keepdims=True)
    live = iota((slots, 1), 0) < fcv[...]
    behind = lax.rem(me - lax.div(sources, clusters) + n_cl, n_cl)
    picked_row = jnp.where(live, behind * clusters + lax.rem(sources, clusters), -1)
    one_hot = jnp.where(iota((slots, all_cl), 1) == picked_row, 1.0, 0.0).astype(bf16)
    slot_shape = (slots, ftv.shape[1])
    mine = iota(slot_shape, 1) == iota(slot_shape, 0) + me * slots
    targets = jnp.sum(jnp.where(mine, ftv[...], 0), axis=1, keepdims=True)
    target_dev = lax.div(targets, clusters)
    target_lane = lax.rem(targets, clusters) == lax.div(iota((slots, wide), 1), ranks)

    gram = jnp.zeros((count, count), f32)
    for t in range(clusters):
        rows = bv[pl.ds(t, count, stride=clusters), :]
        gram += lax.dot_general(
            rows, rows, (((1,), (1,)), ((), ())), precision=lax.Precision.HIGHEST, preferred_element_type=f32
        )
    flat_gram = count * count
    widen = jnp.where(
        iota((count, flat_gram), 0) == lax.rem(iota((count, flat_gram), 1), count), 1.0, 0.0
    ).astype(bf16)
    gram_lane = iota((count, flat_gram), 0) == lax.div(iota((count, flat_gram), 1), count)
    gram_wide = sum(dot(part, widen) for part in parts3(gram))
    ga_send[0] = jnp.sum(jnp.where(gram_lane, gram_wide, 0.0), axis=0, keepdims=True)

    def send_ga(o, _):
        send(ga_send, ga_recv.at[pl.ds(o - 1, 1)], 1, {"cl": lax.rem(me + o, n_cl)}).start()
        return 0

    lax.fori_loop(1, n_cl, send_ga, 0)

    def arrived(ref, which):
        pltpu.make_async_copy(ref, ref, recv_sem.at[which]).wait()

    def left(ref, which):
        pltpu.make_async_copy(ref, ref, send_sem.at[which]).wait()

    arrived(e_recv, 0)
    rows = jnp.concatenate([e_send[...], e_recv[...]], axis=0)
    rows = jnp.where(own_lane[None], jnp.broadcast_to(rows, (n_cl, clusters, wide)), 0.0)
    picked = dot(one_hot, rows.reshape(all_cl, wide).astype(bf16)).astype(bf16)
    product = dot(picked, spread[...]) * cv[...].astype(f32)
    high = product.astype(bf16)
    low = (product - high.astype(f32)).astype(bf16)
    term = dot(high, gather[...]) + dot(low, gather[...])
    term = jnp.where(target_lane, term, 0.0)

    def partial_for(device):
        return jnp.sum(jnp.where(target_dev == device, term, 0.0), axis=0, keepdims=True)

    for i, o in enumerate(offsets):
        p_send[i] = partial_for(lax.rem(me + o, n_cl))
    for i, o in enumerate(offsets):
        send(p_send.at[i], p_recv.at[i], 2, {"cl": lax.rem(me + o, n_cl)}).start()
    own_partial = partial_for(me)

    for i in range(2):
        halos[i].wait_recv()
    loads[6].wait()
    before = jnp.where(me > 0, halo[0], 0.0)
    after = jnp.where(me < n_cl - 1, halo[1], 0.0)
    window = jnp.concatenate([before, current, after], axis=0).astype(bf16)
    reach = window.shape[0]
    listed = lv[...]
    gathered = jnp.concatenate(
        [
            dot(
                jnp.where(iota((clusters, reach), 1) == listed[:, k : k + 1], 1.0, 0.0).astype(bf16), window
            ).astype(bf16)
            for k in range(near_k)
        ],
        axis=1,
    )
    loads[7].wait()
    image = 0.5 * current
    pair = 2
    row_id = iota((clusters, width), 0)
    for t in range(0, clusters, pair):
        blocks = jnp.concatenate(
            [
                jnp.concatenate([nv[(t + u) * near_k + k] for k in range(near_k)], axis=1)
                for u in range(pair)
            ],
            axis=0,
        )
        result = dot_t(gathered, blocks)
        for u in range(pair):
            image += jnp.where(row_id == t + u, result[:, u * width : (u + 1) * width], 0.0)

    arrived(ga_recv, 1)
    group_gram = ga_send[0] + jnp.sum(ga_recv[...], axis=0)
    gb_send[0] = group_gram

    def send_gb(o, _):
        send(gb_send, gb_recv.at[pl.ds(o - 1, 1)], 3, {"grp": lax.rem(grp + o, n_grp)}).start()
        return 0

    lax.fori_loop(1, n_grp, send_gb, 0)

    loads[8].wait()
    arrived(p_recv, 2)
    coupled = own_partial + jnp.sum(p_recv[...], axis=0)
    coupled = jnp.where(own_lane, jnp.broadcast_to(coupled, (clusters, wide)), 0.0).astype(bf16)
    image += dot(coupled, tbv[...])

    basis3 = bv[...].reshape(count, clusters, width)
    sums = jnp.sum(basis3 * image[None], axis=1)
    squares = jnp.sum(image * image, axis=0, keepdims=True)
    tail = jnp.where(iota((8, width), 0) == 0, squares, 0.0)
    stacked = jnp.concatenate([sums, tail, jnp.zeros((width - count - 8, width), f32)], axis=0)
    ones = jnp.ones((8, width), bf16)
    row = sum(dot_t(ones, part) for part in parts3(stacked))[0:1]
    r_send[0] = row

    def send_r(o, _):
        send(r_send, r_recv.at[pl.ds(o - 1, 1)], 4, far_device(o)).start()
        return 0

    lax.fori_loop(1, total, send_r, 0)

    arrived(gb_recv, 3)
    whole_gram = gb_send[0] + jnp.sum(gb_recv[...], axis=0)
    narrow = jnp.where(
        lax.rem(iota((flat_gram, width), 0), count) == iota((flat_gram, width), 1), 1.0, 0.0
    ).astype(bf16)
    gram_rows = jnp.where(gram_lane, jnp.broadcast_to(whole_gram, (count, flat_gram)), 0.0)
    gram_full = sum(dot(part, narrow) for part in parts3(gram_rows))

    arrived(r_recv, 4)
    inverse = 1.0 / float(total * clusters * width)
    mean = (r_send[0] + jnp.sum(r_recv[...], axis=0)) * inverse
    diagonal = iota((count, width), 0) == iota((count, width), 1)
    projection = jnp.sum(jnp.where(diagonal, mean, 0.0), axis=1, keepdims=True)
    applied = jnp.sum(gram_full * mean, axis=1, keepdims=True) * inverse
    lane = iota((1, width), 1)
    image_mean = jnp.sum(jnp.where(lane == count, mean, 0.0), axis=1, keepdims=True)
    change = jnp.sum(projection * (applied - 2.0 * projection), axis=0, keepdims=True)
    norm = jnp.sqrt(image_mean + change + 1e-06)
    spread_p = jnp.broadcast_to(projection, (count, width))
    remainder = image - jnp.sum(basis3 * spread_p[:, None, :], axis=0)
    out_ref[...] = remainder * (1.0 / norm)
    hess_ref[...] = jnp.where(lane == count, norm, mean)[:, : count + 1]

    for i in range(2):
        halos[i].wait_send()
    left(e_recv, 0)
    left(ga_recv, 1)
    left(p_recv, 2)
    left(gb_recv, 3)
    left(r_recv, 4)


def on_device(n_cl, n_grp, basis, near_blocks, near_list, source_basis, target_basis, coupling, far_target, far_source, far_count):
    count, _, clusters, width = basis.shape
    near_k = near_blocks.shape[2]
    ranks = source_basis.shape[2]
    slots = coupling.shape[1]
    wide = clusters * ranks
    square = ranks * ranks
    total = n_cl * n_grp
    offsets = target_offsets(n_cl)
    args = (
        basis.reshape(count * clusters, width),
        near_blocks.reshape(clusters * near_k, width, width),
        near_list.reshape(clusters, near_k),
        source_basis.reshape(wide, width),
        target_basis.reshape(wide, width),
        coupling.reshape(slots, square),
        far_target,
        far_source,
        far_count,
    )
    f32, bf16 = jnp.float32, jnp.bfloat16
    order = (0, 1, 2, 3, 4, 5, 6, 7, 8)
    next_vector, hessenberg = pl.pallas_call(
        functools.partial(kernel, n_cl, n_grp, offsets),
        out_shape=(
            jax.ShapeDtypeStruct((clusters, width), f32),
            jax.ShapeDtypeStruct((1, count + 1), f32),
        ),
        in_specs=[pl.BlockSpec(memory_space=pl.ANY)] * len(args),
        out_specs=(pl.BlockSpec(memory_space=pltpu.VMEM), pl.BlockSpec(memory_space=pltpu.VMEM)),
        scratch_shapes=[pltpu.VMEM(args[i].shape, args[i].dtype) for i in order]
        + [
            pltpu.VMEM((wide, square), bf16),
            pltpu.VMEM((square, wide), bf16),
            pltpu.VMEM((1, 1, wide), f32),
            pltpu.VMEM((n_cl - 1, 1, wide), f32),
            pltpu.VMEM((2, clusters, width), f32),
            pltpu.VMEM((len(offsets), 1, wide), f32),
            pltpu.VMEM((len(offsets), 1, wide), f32),
            pltpu.VMEM((1, 1, count * count), f32),
            pltpu.VMEM((n_cl - 1, 1, count * count), f32),
            pltpu.VMEM((1, 1, count * count), f32),
            pltpu.VMEM((n_grp - 1, 1, count * count), f32),
            pltpu.VMEM((1, 1, width), f32),
            pltpu.VMEM((total - 1, 1, width), f32),
            pltpu.SemaphoreType.DMA((9,)),
            pltpu.SemaphoreType.DMA((4,)),
            pltpu.SemaphoreType.DMA((5,)),
            pltpu.SemaphoreType.DMA((5,)),
        ],
        compiler_params=pltpu.CompilerParams(collective_id=0, has_side_effects=True),
        name="arnoldi_step",
    )(*args)
    return next_vector.reshape(1, clusters, width), hessenberg.reshape(count + 1)


def solution(mesh):
    placed = (
        P(None, "grp", "cl", None),
        P("grp", "cl", None, None, None),
        P("grp", "cl", None),
        P("grp", "cl", None, None),
        P("grp", "cl", None, None),
        P("grp", "cl", None),
        P("grp", None),
        P("grp", "cl"),
        P("grp", "cl"),
    )
    return jax.shard_map(
        functools.partial(on_device, mesh.shape["cl"], mesh.shape["grp"]),
        mesh=mesh,
        in_specs=placed,
        out_specs=(P("grp", "cl", None), P()),
        check_vma=False,
    )
```

time: 123 us -> 24 us (0.20); the launches traced: 121 us -> 23.8 us
  blocking collectives: 100 us -> 0 us
  Pallas kernels: 0 us -> 19.3 us
  starting transfers between devices: 6.15 us -> 0 us
  matrix products: 3.17 us -> 0 us
  between operations: 4.13 us -> 1.3 us
  other arithmetic: 2.44 us -> 0 us
  local copies, waits for them, and re-layouts: 4.96 us -> 3.13 us
    psum x1 -> x0, blocking collectives: 37 us -> none  [on_device(): lax.psum((local_products, jnp.sum(flat_image * flat_image), gram_local),...]
    unnamed x1 -> x0, blocking collectives: 34.8 us -> none
    all_gather x1 -> x0, blocking collectives: 28.6 us -> none  [on_device(): all_expansion = lax.all_gather(expansion, 'cl', axis=0, tiled=True)]
    pallas_call x0 -> x1, Pallas kernels: none -> 19.3 us  [on_device(): pl.pallas_call(functools.partial(kernel, n_cl, n_grp, offsets), out_shape...]
    ppermute x2 -> x0, starting transfers between devices: 6.15 us -> none  [the longest x1 4.86 us: with_halo(): lax.ppermute(tail, axis, [(i, (i + 1) % count) for i in range(ends)])]
    dot_general x9 -> x0, matrix products: 3.17 us -> none  [the longest x1 0.98 us: on_device(): jnp.einsum('srp,sp->sr', source_basis[0], current_bf, preferred_element_t...]
    unnamed x17 -> x8, local copies, waits for them, and re-layouts: 2.62 us -> 2.46 us
  transfers between devices with their start and end apart: 2 -> 0, of which waited for: 0 -> 0; matrix products, arithmetic and copies ran while one was open for 3% -> 0% of each run, Pallas kernels for 0% -> 0%
where the time goes in v1:
time: 24 us; the launch traced here: 23.8 us
  Pallas kernels  19.3 us (80%)
  local copies, waits for them, and re-layouts  3.13 us (13%)
  between operations  1.3 us (5%)
    pallas_call x1, Pallas kernels, on_device(): pl.pallas_call(functools.partial(kernel, n_cl, n_grp, offsets), out_shape...  19.3 us
    unnamed x8, local copies, waits for them, and re-layouts  2.46 us
    reshape x1, local copies, waits for them, and re-layouts, on_device(): near_list.reshape(clusters, near_k)  0.67 us

profile of v1, /device:TPU:0, one launch (start us, length us, event | category | flops | bytes accessed | tf_op | source)
XLA Modules:
  0.0 23.8 jit_solution(14238489191820087560)
XLA Ops:
  1.3 0.0 copy-start.1
  1.3 0.7 %copy-done.1 = s32[1,8,4]{1,2,0:T(4,128)S(1)} copy-done((s32[1,8,4]{1,2,0:T(4,128)S(1)}, s32[1,8,4]{1,2,0:T(4,128)}, u32[]{:S(2)}) %copy-start.1) | copy-done | bytes 152
  2.0 0.7 %copy.11.list_h = s32[8,4]{1,0:T(8,128)} copy(s32[8,4]{0,1:T(4,128)S(1)} %bitcast.14) | data formatting | bytes 256 | tf_op jit(solution)/shard_map/reshape | solution.py:339
  2.6 19.3 %arnoldi_step.1 = (f32[8,128]{1,0:T(8,128)}, f32[1,17]{1,0:T(1,128)}) custom-call(f32[128,128]{1,0:T(8,128)} %bitcast.9, bf16[32,128,128]{2,1,0:T(8,128)(2,1)} %bitcast.8, s32[8,4]{1,0:T(8,128)} %copy.11.list_h, bf16[256,128]{1,0:T(8,128)(2,1)} %bitcast.10, bf16[256,128]{1,0:T(8,128)(2,1)} %bitcast.11, bf16[16,1024]{1,0:T(8,128)(2,1)} %bitcast.12, ...), custom_call_target="tpu_custom_call" | custom-call | tf_op jit(solution)/shard_map/arnoldi_step/pallas_call | solution.py:349
  22.0 0.0 copy-start
  22.0 0.7 %copy-done = f32[8,128]{1,0:T(8,128)S(1)} copy-done((f32[8,128]{1,0:T(8,128)S(1)}, f32[8,128]{1,0:T(8,128)}, u32[]{:S(2)}) %copy-start) | copy-done | bytes 4120
  22.7 0.0 copy-start.2
  22.7 0.6 %copy.15 = f32[1,8,128]{2,1,0:T(8,128)} copy(f32[1,8,128]{2,1,0:T(8,128)S(1)} %bitcast.13) | data formatting | bytes 8192
  23.2 0.0 copy-done.2
  23.3 0.5 %copy.16 = f32[17]{0:T(128)} copy(f32[17]{0:T(128)S(1)} %bitcast.15) | data formatting | bytes 136
Async XLA Ops:
  1.3 0.7 %copy-start.1 = (s32[1,8,4]{1,2,0:T(4,128)S(1)}, s32[1,8,4]{1,2,0:T(4,128)}, u32[]{:S(2)}) copy-start(s32[1,8,4]{1,2,0:T(4,128)} %param.11) | copy-start | bytes 388
  22.0 0.7 %copy-start = (f32[8,128]{1,0:T(8,128)S(1)}, f32[8,128]{1,0:T(8,128)}, u32[]{:S(2)}) copy-start(f32[8,128]{1,0:T(8,128)} %get-tuple-element.4) | copy-start | bytes 12292
  22.7 0.6 %copy-start.2 = (f32[1,17]{1,0:T(1,128)S(1)}, f32[1,17]{1,0:T(1,128)}, u32[]{:S(2)}) copy-start(f32[1,17]{1,0:T(1,128)} %get-tuple-element.5) | copy-start | bytes 208

commit v2 on v1

--- a/solution.py
+++ b/solution.py
@@ -18,6 +18,34 @@
 
 def iota(shape, dim):
     return lax.broadcasted_iota(jnp.int32, shape, dim)
+
+
+def power_of_two(n):
+    return n & (n - 1) == 0
+
+
+def quot(x, n):
+    return lax.shift_right_logical(x, n.bit_length() - 1) if power_of_two(n) else lax.div(x, n)
+
+
+def rest(x, n):
+    return x & (n - 1) if power_of_two(n) else lax.rem(x, n)
+
+
+def partner(me, o, n):
+    return me ^ o if power_of_two(n) else lax.rem(me + o, n)
+
+
+def place_of(me, device, n):
+    return me ^ device if power_of_two(n) else lax.rem(me - device + n, n)
+
+
+def for_others(n, body):
+    if n <= 64:
+        for o in range(1, n):
+            body(o)
+    else:
+        pl.loop(1, n)(body)
 
 
 def parts3(x):
@@ -82,7 +110,7 @@
     me, grp = lax.axis_index("cl"), lax.axis_index("grp")
     total = n_cl * n_grp
     flat_me = me * n_grp + grp
-    clusters, near_k = lv.shape
+    near_k, clusters = lv.shape
     width = bv.shape[1]
     count = bv.shape[0] // clusters
     slots = cv.shape[0]
@@ -93,13 +121,13 @@
     barrier = pltpu.get_barrier_semaphore()
 
     def far_device(o):
-        flat = lax.rem(flat_me + o, total)
-        return {"cl": lax.div(flat, n_grp), "grp": lax.rem(flat, n_grp)}
-
-    def greet(o, _):
+        flat = partner(flat_me, o, total)
+        return {"cl": quot(flat, n_grp), "grp": rest(flat, n_grp)}
+
+    def greet(o):
         pl.semaphore_signal(barrier, inc=1, device_id=far_device(o), device_id_type=MESH)
-        return 0
-
+
+    for_others(total, greet)
     loads = [
         pltpu.make_async_copy(src, dst, local_sem.at[i])
         for i, (src, dst) in enumerate(
@@ -118,13 +146,12 @@
     ]
     for load in loads:
         load.start()
-    lax.fori_loop(1, total, greet, 0)
 
     loads[0].wait()
     loads[1].wait()
     current = bv[(count - 1) * clusters :, :]
     current_bf = current.astype(bf16)
-    own_lane = iota((clusters, wide), 0) == lax.div(iota((clusters, wide), 1), ranks)
+    own_lane = iota((clusters, wide), 0) == quot(iota((clusters, wide), 1), ranks)
     e8 = jnp.where(own_lane, dot_t(current_bf, sbv[...]), 0.0)
     e_send[0] = jnp.sum(e8, axis=0, keepdims=True).astype(bf16).astype(f32)
 
@@ -140,11 +167,10 @@
             device_id_type=MESH,
         )
 
-    def send_e(o, _):
-        send(e_send, e_recv.at[pl.ds(o - 1, 1)], 0, {"cl": lax.rem(me + o, n_cl)}).start()
-        return 0
-
-    lax.fori_loop(1, n_cl, send_e, 0)
+    def send_e(o):
+        send(e_send, e_recv.at[pl.ds(o - 1, 1)], 0, {"cl": partner(me, o, n_cl)}).start()
+
+    for_others(n_cl, send_e)
     tile = bv.at[pl.ds((count - 1) * clusters, clusters)]
     halos = [
         pltpu.make_async_remote_copy(
@@ -152,7 +178,7 @@
             dst_ref=halo.at[i],
             send_sem=halo_sem.at[i],
             recv_sem=halo_sem.at[2 + i],
-            device_id={"cl": lax.rem(me + shift, n_cl)},
+            device_id={"cl": rest(me + shift, n_cl)},
             device_id_type=MESH,
         )
         for i, shift in enumerate((1, n_cl - 1))
@@ -160,28 +186,28 @@
     for copy in halos:
         copy.start()
 
-    def fill(ref, test):
-        step = 128
-        for at in range(0, ref.shape[0], step):
-            block = (step, ref.shape[1])
-            ref[at : at + step, :] = jnp.where(test(iota(block, 0) + at, iota(block, 1)), 1.0, 0.0).astype(bf16)
-
-    fill(spread, lambda r, c: lax.rem(r, ranks) == lax.rem(c, ranks))
-    fill(gather, lambda r, c: lax.div(r, ranks) == lax.rem(c, ranks))
+    repeat = jnp.where(
+        iota((ranks, ranks * ranks), 0) == rest(iota((ranks, ranks * ranks), 1), ranks), 1.0, 0.0
+    ).astype(bf16)
+    for at in range(0, wide, ranks):
+        spread[at : at + ranks, :] = repeat
+    lane_rank = rest(iota((ranks, wide), 1), ranks)
+    for r in range(ranks):
+        gather[r * ranks : (r + 1) * ranks, :] = jnp.where(lane_rank == r, 1.0, 0.0).astype(bf16)
 
     for load in loads[2:6]:
         load.wait()
     eye = iota((slots, slots), 0) == iota((slots, slots), 1)
     sources = jnp.sum(jnp.where(eye, fsv[...], 0), axis=1, keepdims=True)
     live = iota((slots, 1), 0) < fcv[...]
-    behind = lax.rem(me - lax.div(sources, clusters) + n_cl, n_cl)
-    picked_row = jnp.where(live, behind * clusters + lax.rem(sources, clusters), -1)
+    behind = place_of(me, quot(sources, clusters), n_cl)
+    picked_row = jnp.where(live, behind * clusters + rest(sources, clusters), -1)
     one_hot = jnp.where(iota((slots, all_cl), 1) == picked_row, 1.0, 0.0).astype(bf16)
     slot_shape = (slots, ftv.shape[1])
     mine = iota(slot_shape, 1) == iota(slot_shape, 0) + me * slots
     targets = jnp.sum(jnp.where(mine, ftv[...], 0), axis=1, keepdims=True)
-    target_dev = lax.div(targets, clusters)
-    target_lane = lax.rem(targets, clusters) == lax.div(iota((slots, wide), 1), ranks)
+    target_dev = quot(targets, clusters)
+    target_lane = rest(targets, clusters) == quot(iota((slots, wide), 1), ranks)
 
     gram = jnp.zeros((count, count), f32)
     for t in range(clusters):
@@ -191,17 +217,16 @@
         )
     flat_gram = count * count
     widen = jnp.where(
-        iota((count, flat_gram), 0) == lax.rem(iota((count, flat_gram), 1), count), 1.0, 0.0
+        iota((count, flat_gram), 0) == rest(iota((count, flat_gram), 1), count), 1.0, 0.0
     ).astype(bf16)
-    gram_lane = iota((count, flat_gram), 0) == lax.div(iota((count, flat_gram), 1), count)
+    gram_lane = iota((count, flat_gram), 0) == quot(iota((count, flat_gram), 1), count)
     gram_wide = sum(dot(part, widen) for part in parts3(gram))
     ga_send[0] = jnp.sum(jnp.where(gram_lane, gram_wide, 0.0), axis=0, keepdims=True)
 
-    def send_ga(o, _):
-        send(ga_send, ga_recv.at[pl.ds(o - 1, 1)], 1, {"cl": lax.rem(me + o, n_cl)}).start()
-        return 0
-
-    lax.fori_loop(1, n_cl, send_ga, 0)
+    def send_ga(o):
+        send(ga_send, ga_recv.at[pl.ds(o - 1, 1)], 1, {"cl": partner(me, o, n_cl)}).start()
+
+    for_others(n_cl, send_ga)
 
     def arrived(ref, which):
         pltpu.make_async_copy(ref, ref, recv_sem.at[which]).wait()
@@ -223,9 +248,9 @@
         return jnp.sum(jnp.where(target_dev == device, term, 0.0), axis=0, keepdims=True)
 
     for i, o in enumerate(offsets):
-        p_send[i] = partial_for(lax.rem(me + o, n_cl))
+        p_send[i] = partial_for(rest(me + o, n_cl))
     for i, o in enumerate(offsets):
-        send(p_send.at[i], p_recv.at[i], 2, {"cl": lax.rem(me + o, n_cl)}).start()
+        send(p_send.at[i], p_recv.at[i], 2, {"cl": rest(me + o, n_cl)}).start()
     own_partial = partial_for(me)
 
     for i in range(2):
@@ -235,11 +260,14 @@
     after = jnp.where(me < n_cl - 1, halo[1], 0.0)
     window = jnp.concatenate([before, current, after], axis=0).astype(bf16)
     reach = window.shape[0]
-    listed = lv[...]
+    turn = iota((clusters, clusters), 0) == iota((clusters, clusters), 1)
+    listed = [
+        jnp.sum(jnp.where(turn, lv[k : k + 1, :], 0), axis=1, keepdims=True) for k in range(near_k)
+    ]
     gathered = jnp.concatenate(
         [
             dot(
-                jnp.where(iota((clusters, reach), 1) == listed[:, k : k + 1], 1.0, 0.0).astype(bf16), window
+                jnp.where(iota((clusters, reach), 1) == listed[k], 1.0, 0.0).astype(bf16), window
             ).astype(bf16)
             for k in range(near_k)
         ],
@@ -265,11 +293,10 @@
     group_gram = ga_send[0] + jnp.sum(ga_recv[...], axis=0)
     gb_send[0] = group_gram
 
-    def send_gb(o, _):
-        send(gb_send, gb_recv.at[pl.ds(o - 1, 1)], 3, {"grp": lax.rem(grp + o, n_grp)}).start()
-        return 0
-
-    lax.fori_loop(1, n_grp, send_gb, 0)
+    def send_gb(o):
+        send(gb_send, gb_recv.at[pl.ds(o - 1, 1)], 3, {"grp": partner(grp, o, n_grp)}).start()
+
+    for_others(n_grp, send_gb)
 
     loads[8].wait()
     arrived(p_recv, 2)
@@ -286,16 +313,15 @@
     row = sum(dot_t(ones, part) for part in parts3(stacked))[0:1]
     r_send[0] = row
 
-    def send_r(o, _):
+    def send_r(o):
         send(r_send, r_recv.at[pl.ds(o - 1, 1)], 4, far_device(o)).start()
-        return 0
-
-    lax.fori_loop(1, total, send_r, 0)
+
+    for_others(total, send_r)
 
     arrived(gb_recv, 3)
     whole_gram = gb_send[0] + jnp.sum(gb_recv[...], axis=0)
     narrow = jnp.where(
-        lax.rem(iota((flat_gram, width), 0), count) == iota((flat_gram, width), 1), 1.0, 0.0
+        rest(iota((flat_gram, width), 0), count) == iota((flat_gram, width), 1), 1.0, 0.0
     ).astype(bf16)
     gram_rows = jnp.where(gram_lane, jnp.broadcast_to(whole_gram, (count, flat_gram)), 0.0)
     gram_full = sum(dot(part, narrow) for part in parts3(gram_rows))
@@ -324,6 +350,17 @@
     left(r_recv, 4)
 
 
+def hand_out(vector, column, vector_h, column_h, sem):
+    copies = [
+        pltpu.make_async_copy(vector, vector_h, sem.at[0]),
+        pltpu.make_async_copy(column, column_h, sem.at[1]),
+    ]
+    for copy in copies:
+        copy.start()
+    for copy in copies:
+        copy.wait()
+
+
 def on_device(n_cl, n_grp, basis, near_blocks, near_list, source_basis, target_basis, coupling, far_target, far_source, far_count):
     count, _, clusters, width = basis.shape
     near_k = near_blocks.shape[2]
@@ -336,7 +373,7 @@
     args = (
         basis.reshape(count * clusters, width),
         near_blocks.reshape(clusters * near_k, width, width),
-        near_list.reshape(clusters, near_k),
+        near_list.reshape(clusters, near_k).T,
         source_basis.reshape(wide, width),
         target_basis.reshape(wide, width),
         coupling.reshape(slots, square),
@@ -349,8 +386,8 @@
     next_vector, hessenberg = pl.pallas_call(
         functools.partial(kernel, n_cl, n_grp, offsets),
         out_shape=(
-            jax.ShapeDtypeStruct((clusters, width), f32),
-            jax.ShapeDtypeStruct((1, count + 1), f32),
+            pltpu.VMEM((clusters, width), f32),
+            pltpu.VMEM((1, count + 1), f32),
         ),
         in_specs=[pl.BlockSpec(memory_space=pl.ANY)] * len(args),
         out_specs=(pl.BlockSpec(memory_space=pltpu.VMEM), pl.BlockSpec(memory_space=pltpu.VMEM)),
@@ -377,6 +414,19 @@
         compiler_params=pltpu.CompilerParams(collective_id=0, has_side_effects=True),
         name="arnoldi_step",
     )(*args)
+    next_vector = pltpu.with_memory_space_constraint(next_vector, pltpu.VMEM)
+    hessenberg = pltpu.with_memory_space_constraint(hessenberg, pltpu.VMEM)
+    next_vector, hessenberg = pl.pallas_call(
+        hand_out,
+        out_shape=(
+            jax.ShapeDtypeStruct((clusters, width), f32),
+            jax.ShapeDtypeStruct((1, count + 1), f32),
+        ),
+        in_specs=[pl.BlockSpec(memory_space=pltpu.VMEM)] * 2,
+        out_specs=(pl.BlockSpec(memory_space=pl.ANY), pl.BlockSpec(memory_space=pl.ANY)),
+        scratch_shapes=[pltpu.SemaphoreType.DMA((2,))],
+        name="hand_out",
+    )(next_vector, hessenberg)
     return next_vector.reshape(1, clusters, width), hessenberg.reshape(count + 1)
 
 

time: 24 us -> 21.2 us (0.88)
  local copies, waits for them, and re-layouts: 3.13 us -> 0 us
  Pallas kernels: 19.3 us -> 19.8 us
    unnamed x8 -> x0, local copies, waits for them, and re-layouts: 2.46 us -> none
    reshape x1 -> x0, local copies, waits for them, and re-layouts: 0.67 us -> none  [on_device(): near_list.reshape(clusters, near_k)]
    pallas_call x0 -> x1, Pallas kernels: none -> 0.61 us  [on_device(): pl.pallas_call(hand_out, out_shape=(jax.ShapeDtypeStruct((clusters, width...]
where the time goes in v2:
time: 21.2 us; the launch traced here: 21.1 us
  Pallas kernels  19.8 us (93%)
  between operations  1.29 us (6%)
    pallas_call x1, Pallas kernels, on_device(): pl.pallas_call(functools.partial(kernel, n_cl, n_grp, offsets), out_shape...  19.2 us
    pallas_call x1, Pallas kernels, on_device(): pl.pallas_call(hand_out, out_shape=(jax.ShapeDtypeStruct((clusters, width...  0.61 us

profile of v2, /device:TPU:0, one launch (start us, length us, event | category | flops | bytes accessed | tf_op | source)
XLA Modules:
  0.0 21.1 jit_solution(7041353030332420285)
XLA Ops:
  1.3 19.2 %arnoldi_step.1 = (f32[8,128]{1,0:T(8,128)S(1)}, f32[1,17]{1,0:T(1,128)S(1)}) custom-call(f32[128,128]{1,0:T(8,128)} %bitcast.11, bf16[32,128,128]{2,1,0:T(8,128)(2,1)} %bitcast.10, s32[4,8]{1,0:T(4,128)} %bitcast.15, bf16[256,128]{1,0:T(8,128)(2,1)} %bitcast.12, bf16[256,128]{1,0:T(8,128)(2,1)} %bitcast.13, bf16[16,1024]{1,0:T(8,128)(2,1)} %bitcast.14, ...), custom_call_target="tpu_custom_call" | custom-call | tf_op jit(solution)/shard_map/arnoldi_step/pallas_call | solution.py:386
  20.5 0.6 %hand_out.1 = (f32[8,128]{1,0:T(8,128)}, f32[1,17]{1,0:T(1,128)}) custom-call(f32[8,128]{1,0:T(8,128)S(1)} %get-tuple-element.6.vector, f32[1,17]{1,0:T(1,128)S(1)} %get-tuple-element.7.column), custom_call_target="tpu_custom_call" | custom-call | tf_op jit(solution)/shard_map/hand_out/pallas_call | solution.py:419

commit v3 on v2

--- a/solution.py
+++ b/solution.py
@@ -42,7 +42,7 @@
 
 def for_others(n, body):
     if n <= 64:
-        for o in range(1, n):
+        for o in reversed(range(1, n)):
             body(o)
     else:
         pl.loop(1, n)(body)
@@ -124,10 +124,15 @@
         flat = partner(flat_me, o, total)
         return {"cl": quot(flat, n_grp), "grp": rest(flat, n_grp)}
 
-    def greet(o):
-        pl.semaphore_signal(barrier, inc=1, device_id=far_device(o), device_id_type=MESH)
-
-    for_others(total, greet)
+    def greet(axis, mine, n):
+        def one(o):
+            device = {axis: partner(mine, o, n)}
+            pl.semaphore_signal(barrier, inc=1, device_id=device, device_id_type=MESH)
+
+        for_others(n, one)
+
+    greet("cl", me, n_cl)
+    greet("grp", grp, n_grp)
     loads = [
         pltpu.make_async_copy(src, dst, local_sem.at[i])
         for i, (src, dst) in enumerate(
@@ -155,7 +160,44 @@
     e8 = jnp.where(own_lane, dot_t(current_bf, sbv[...]), 0.0)
     e_send[0] = jnp.sum(e8, axis=0, keepdims=True).astype(bf16).astype(f32)
 
-    pl.semaphore_wait(barrier, total - 1)
+    repeat = jnp.where(
+        iota((ranks, ranks * ranks), 0) == rest(iota((ranks, ranks * ranks), 1), ranks), 1.0, 0.0
+    ).astype(bf16)
+    for at in range(0, wide, ranks):
+        spread[at : at + ranks, :] = repeat
+    lane_rank = rest(iota((ranks, wide), 1), ranks)
+    for r in range(ranks):
+        gather[r * ranks : (r + 1) * ranks, :] = jnp.where(lane_rank == r, 1.0, 0.0).astype(bf16)
+
+    for load in loads[2:6]:
+        load.wait()
+    eye = iota((slots, slots), 0) == iota((slots, slots), 1)
+    sources = jnp.sum(jnp.where(eye, fsv[...], 0), axis=1, keepdims=True)
+    live = iota((slots, 1), 0) < fcv[...]
+    behind = place_of(me, quot(sources, clusters), n_cl)
+    picked_row = jnp.where(live, behind * clusters + rest(sources, clusters), -1)
+    one_hot = jnp.where(iota((slots, all_cl), 1) == picked_row, 1.0, 0.0).astype(bf16)
+    slot_shape = (slots, ftv.shape[1])
+    mine = iota(slot_shape, 1) == iota(slot_shape, 0) + me * slots
+    targets = jnp.sum(jnp.where(mine, ftv[...], 0), axis=1, keepdims=True)
+    target_dev = quot(targets, clusters)
+    target_lane = rest(targets, clusters) == quot(iota((slots, wide), 1), ranks)
+
+    gram = jnp.zeros((count, count), f32)
+    for t in range(clusters):
+        rows = bv[pl.ds(t, count, stride=clusters), :]
+        gram += lax.dot_general(
+            rows, rows, (((1,), (1,)), ((), ())), precision=lax.Precision.HIGHEST, preferred_element_type=f32
+        )
+    flat_gram = count * count
+    widen = jnp.where(
+        iota((count, flat_gram), 0) == rest(iota((count, flat_gram), 1), count), 1.0, 0.0
+    ).astype(bf16)
+    gram_lane = iota((count, flat_gram), 0) == quot(iota((count, flat_gram), 1), count)
+    gram_wide = sum(dot(part, widen) for part in parts3(gram))
+    ga_send[0] = jnp.sum(jnp.where(gram_lane, gram_wide, 0.0), axis=0, keepdims=True)
+
+    pl.semaphore_wait(barrier, n_cl + n_grp - 2)
 
     def send(src, dst, which, device):
         return pltpu.make_async_remote_copy(
@@ -186,43 +228,6 @@
     for copy in halos:
         copy.start()
 
-    repeat = jnp.where(
-        iota((ranks, ranks * ranks), 0) == rest(iota((ranks, ranks * ranks), 1), ranks), 1.0, 0.0
-    ).astype(bf16)
-    for at in range(0, wide, ranks):
-        spread[at : at + ranks, :] = repeat
-    lane_rank = rest(iota((ranks, wide), 1), ranks)
-    for r in range(ranks):
-        gather[r * ranks : (r + 1) * ranks, :] = jnp.where(lane_rank == r, 1.0, 0.0).astype(bf16)
-
-    for load in loads[2:6]:
-        load.wait()
-    eye = iota((slots, slots), 0) == iota((slots, slots), 1)
-    sources = jnp.sum(jnp.where(eye, fsv[...], 0), axis=1, keepdims=True)
-    live = iota((slots, 1), 0) < fcv[...]
-    behind = place_of(me, quot(sources, clusters), n_cl)
-    picked_row = jnp.where(live, behind * clusters + rest(sources, clusters), -1)
-    one_hot = jnp.where(iota((slots, all_cl), 1) == picked_row, 1.0, 0.0).astype(bf16)
-    slot_shape = (slots, ftv.shape[1])
-    mine = iota(slot_shape, 1) == iota(slot_shape, 0) + me * slots
-    targets = jnp.sum(jnp.where(mine, ftv[...], 0), axis=1, keepdims=True)
-    target_dev = quot(targets, clusters)
-    target_lane = rest(targets, clusters) == quot(iota((slots, wide), 1), ranks)
-
-    gram = jnp.zeros((count, count), f32)
-    for t in range(clusters):
-        rows = bv[pl.ds(t, count, stride=clusters), :]
-        gram += lax.dot_general(
-            rows, rows, (((1,), (1,)), ((), ())), precision=lax.Precision.HIGHEST, preferred_element_type=f32
-        )
-    flat_gram = count * count
-    widen = jnp.where(
-        iota((count, flat_gram), 0) == rest(iota((count, flat_gram), 1), count), 1.0, 0.0
-    ).astype(bf16)
-    gram_lane = iota((count, flat_gram), 0) == quot(iota((count, flat_gram), 1), count)
-    gram_wide = sum(dot(part, widen) for part in parts3(gram))
-    ga_send[0] = jnp.sum(jnp.where(gram_lane, gram_wide, 0.0), axis=0, keepdims=True)
-
     def send_ga(o):
         send(ga_send, ga_recv.at[pl.ds(o - 1, 1)], 1, {"cl": partner(me, o, n_cl)}).start()
 
@@ -241,7 +246,8 @@
     product = dot(picked, spread[...]) * cv[...].astype(f32)
     high = product.astype(bf16)
     low = (product - high.astype(f32)).astype(bf16)
-    term = dot(high, gather[...]) + dot(low, gather[...])
+    both = dot(jnp.concatenate([high, low], axis=0), gather[...])
+    term = both[:slots] + both[slots:]
     term = jnp.where(target_lane, term, 0.0)
 
     def partial_for(device):

time: 21.2 us -> 21.3 us (level)
  no operation moved by 1% of the time
where the time goes in v3:
time: 21.3 us; the launch traced here: 21.1 us
  Pallas kernels  19.8 us (93%)
  between operations  1.29 us (6%)
    pallas_call x1, Pallas kernels, on_device(): pl.pallas_call(functools.partial(kernel, n_cl, n_grp, offsets), out_shape...  19.2 us
    pallas_call x1, Pallas kernels, on_device(): pl.pallas_call(hand_out, out_shape=(jax.ShapeDtypeStruct((clusters, width...  0.61 us

profile of v3, /device:TPU:0, one launch (start us, length us, event | category | flops | bytes accessed | tf_op | source)
XLA Modules:
  0.0 21.1 jit_solution(17914906207592958197)
XLA Ops:
  1.3 19.2 %arnoldi_step.1 = (f32[8,128]{1,0:T(8,128)S(1)}, f32[1,17]{1,0:T(1,128)S(1)}) custom-call(f32[128,128]{1,0:T(8,128)} %bitcast.11, bf16[32,128,128]{2,1,0:T(8,128)(2,1)} %bitcast.10, s32[4,8]{1,0:T(4,128)} %bitcast.15, bf16[256,128]{1,0:T(8,128)(2,1)} %bitcast.12, bf16[256,128]{1,0:T(8,128)(2,1)} %bitcast.13, bf16[16,1024]{1,0:T(8,128)(2,1)} %bitcast.14, ...), custom_call_target="tpu_custom_call" | custom-call | tf_op jit(solution)/shard_map/arnoldi_step/pallas_call | solution.py:392
  20.5 0.6 %hand_out.1 = (f32[8,128]{1,0:T(8,128)}, f32[1,17]{1,0:T(1,128)}) custom-call(f32[8,128]{1,0:T(8,128)S(1)} %get-tuple-element.6.vector, f32[1,17]{1,0:T(1,128)S(1)} %get-tuple-element.7.column), custom_call_target="tpu_custom_call" | custom-call | tf_op jit(solution)/shard_map/hand_out/pallas_call | solution.py:425

commit v4 on v2

--- a/solution.py
+++ b/solution.py
@@ -13,7 +13,7 @@
 
 def target_offsets(n_cl):
     near = {o % n_cl for r in range(1, TARGET_REACH + 1) for o in (r, -r)}
-    return sorted((near | {n_cl // 2}) - {0})
+    return sorted((near | {n_cl // 2}) - {0}, key=lambda o: -min(o, n_cl - o))
 
 
 def iota(shape, dim):
@@ -42,7 +42,7 @@
 
 def for_others(n, body):
     if n <= 64:
-        for o in range(1, n):
+        for o in reversed(range(1, n)):
             body(o)
     else:
         pl.loop(1, n)(body)
@@ -124,10 +124,15 @@
         flat = partner(flat_me, o, total)
         return {"cl": quot(flat, n_grp), "grp": rest(flat, n_grp)}
 
-    def greet(o):
-        pl.semaphore_signal(barrier, inc=1, device_id=far_device(o), device_id_type=MESH)
-
-    for_others(total, greet)
+    def greet(axis, mine, n):
+        def one(o):
+            device = {axis: partner(mine, o, n)}
+            pl.semaphore_signal(barrier, inc=1, device_id=device, device_id_type=MESH)
+
+        for_others(n, one)
+
+    greet("cl", me, n_cl)
+    greet("grp", grp, n_grp)
     loads = [
         pltpu.make_async_copy(src, dst, local_sem.at[i])
         for i, (src, dst) in enumerate(
@@ -155,7 +160,7 @@
     e8 = jnp.where(own_lane, dot_t(current_bf, sbv[...]), 0.0)
     e_send[0] = jnp.sum(e8, axis=0, keepdims=True).astype(bf16).astype(f32)
 
-    pl.semaphore_wait(barrier, total - 1)
+    pl.semaphore_wait(barrier, n_cl + n_grp - 2)
 
     def send(src, dst, which, device):
         return pltpu.make_async_remote_copy(
@@ -241,7 +246,8 @@
     product = dot(picked, spread[...]) * cv[...].astype(f32)
     high = product.astype(bf16)
     low = (product - high.astype(f32)).astype(bf16)
-    term = dot(high, gather[...]) + dot(low, gather[...])
+    both = dot(jnp.concatenate([high, low], axis=0), gather[...])
+    term = both[:slots] + both[slots:]
     term = jnp.where(target_lane, term, 0.0)
 
     def partial_for(device):
@@ -308,10 +314,9 @@
     sums = jnp.sum(basis3 * image[None], axis=1)
     squares = jnp.sum(image * image, axis=0, keepdims=True)
     tail = jnp.where(iota((8, width), 0) == 0, squares, 0.0)
-    stacked = jnp.concatenate([sums, tail, jnp.zeros((width - count - 8, width), f32)], axis=0)
-    ones = jnp.ones((8, width), bf16)
-    row = sum(dot_t(ones, part) for part in parts3(stacked))[0:1]
-    r_send[0] = row
+    totals = jnp.sum(jnp.concatenate([sums, tail], axis=0), axis=1, keepdims=True)
+    place = iota((count + 8, width), 0) == iota((count + 8, width), 1)
+    r_send[0] = jnp.sum(jnp.where(place, totals, 0.0), axis=0, keepdims=True)
 
     def send_r(o):
         send(r_send, r_recv.at[pl.ds(o - 1, 1)], 4, far_device(o)).start()

time: 21.2 us -> 20.7 us (0.976)
  Pallas kernels: 19.8 us -> 19.2 us
    pallas_call x1, Pallas kernels: 19.2 us -> 18.6 us  [on_device(): pl.pallas_call(functools.partial(kernel, n_cl, n_grp, offsets), out_shape...]
where the time goes in v4:
time: 20.7 us; the launch traced here: 20.5 us
  Pallas kernels  19.2 us (93%)
  between operations  1.29 us (6%)
    pallas_call x1, Pallas kernels, on_device(): pl.pallas_call(functools.partial(kernel, n_cl, n_grp, offsets), out_shape...  18.6 us
    pallas_call x1, Pallas kernels, on_device(): pl.pallas_call(hand_out, out_shape=(jax.ShapeDtypeStruct((clusters, width...  0.61 us

profile of v4, /device:TPU:0, one launch (start us, length us, event | category | flops | bytes accessed | tf_op | source)
XLA Modules:
  0.0 20.5 jit_solution(12567168316929467552)
XLA Ops:
  1.3 18.6 %arnoldi_step.1 = (f32[8,128]{1,0:T(8,128)S(1)}, f32[1,17]{1,0:T(1,128)S(1)}) custom-call(f32[128,128]{1,0:T(8,128)} %bitcast.11, bf16[32,128,128]{2,1,0:T(8,128)(2,1)} %bitcast.10, s32[4,8]{1,0:T(4,128)} %bitcast.15, bf16[256,128]{1,0:T(8,128)(2,1)} %bitcast.12, bf16[256,128]{1,0:T(8,128)(2,1)} %bitcast.13, bf16[16,1024]{1,0:T(8,128)(2,1)} %bitcast.14, ...), custom_call_target="tpu_custom_call" | custom-call | tf_op jit(solution)/shard_map/arnoldi_step/pallas_call | solution.py:391
  19.9 0.6 %hand_out.1 = (f32[8,128]{1,0:T(8,128)}, f32[1,17]{1,0:T(1,128)}) custom-call(f32[8,128]{1,0:T(8,128)S(1)} %get-tuple-element.6.vector, f32[1,17]{1,0:T(1,128)S(1)} %get-tuple-element.7.column), custom_call_target="tpu_custom_call" | custom-call | tf_op jit(solution)/shard_map/hand_out/pallas_call | solution.py:424
